TPU v7x, 512 devices: a whole 4x8x8 slice. The times are simulated.
512 devices in a mesh: tile: 64 (over z, x, core), tm: 8 (over y).
Axes of the slice: x: 4, y: 8, z: 8, core: 2. Of those that a mesh axis runs over, the one named last changes fastest.
Arguments:
- data: bfloat16 [8192, 64, 128], P('tile', 'tm'), may hold values from -8 to 8
- send_list: int32 [64, 64, 8], P('tile'), may hold values from 0 to 127
- footprint_slot: int32 [8192, 8], P('tile'), may hold values from 0 to 511, as said below
- footprint: bfloat16 [8192, 8, 128], P('tile'), may hold values from 0 to 0.053955078
- colour: int32 [8192], P('tile'), may hold values from 0 to 3, as said below
- correlation: int32 [8192, 8], P('tile'), may hold values from 0 to 8191, as said below
- correlation_gram: float32 [8192, 8], P('tile'), may hold values from 0.01 to 0.15
- traces_init: float32 [64, 8192], P('tm', 'tile'), may hold values from 0 to 4
Outputs:
- traces: float32 [64, 8192], P('tm', 'tile')
- trace_rms: float32 [8192], P('tile')
Inputs may be any that keep to these rules, and one draw needn't show every extreme that they name: footprint_slot[k, j] names the slot c = footprint_slot[k, j] % 8 in which tile device footprint_slot[k, j] // 8 sends a block to the owner of k, tile device k // 128; the 8 slots of one footprint differ. Each tile device owns exactly a quarter of its 128 components in each colour; every listed neighbour has a colour other than the component's own. `correlation`: the tile axis folds the slab's two halves end to end, so the neighbours of a component owned by tile device d are owned by tile device d - 1, d, d + 1 or (d + 32) modulo 64; entries may repeat.
All inputs are finite; a program needn't handle non-finite values.
Results may differ from a plain program's by a relative error of at most 0.0003.
Values may be sent and summed in bfloat16 or wider, within the bound.
A program may use at most 64 MiB of HBM per device.

v0:
```python
import jax
import jax.numpy as jnp
from jax import lax
from jax.sharding import PartitionSpec as P


def shards(
    data, send_list, footprint_slot, footprint, colour, correlation, correlation_gram, traces_init
):
    tile_count = lax.axis_size("tile")
    tile_here = lax.axis_index("tile")
    comp_count = colour.shape[0]
    quarter = comp_count // 4
    frames_dev = data.shape[1]
    voxels = data.shape[2]
    cap_slots = send_list.shape[2]
    slot_count = tile_count * cap_slots
    blocks_fp = footprint.shape[1]
    listed = correlation.shape[1]
    outgoing = data[send_list[0].reshape(-1)].reshape(tile_count, cap_slots, frames_dev, voxels)
    arrived = lax.all_to_all(outgoing, "tile", split_axis=0, concat_axis=0, tiled=True).reshape(
        slot_count, frames_dev, voxels
    )
    weights32 = footprint.astype(jnp.float32)
    self_gram = jnp.sum(weights32 * weights32, axis=(1, 2))
    comp_block = min(32, comp_count)
    block_total = comp_count // comp_block
    slot_range = jnp.arange(slot_count, dtype=jnp.int32)

    def project(inputs):
        slot_ids, weight_rows = inputs
        one_hot = (slot_ids[:, :, None] == slot_range[None, None, :]).astype(jnp.bfloat16)
        spread = jnp.einsum(
            "kjs,kjv->svk", one_hot, weight_rows, preferred_element_type=jnp.bfloat16
        )
        return jnp.einsum("sfv,svk->fk", arrived, spread, preferred_element_type=jnp.float32)

    pieces = lax.map(
        project,
        (
            footprint_slot.reshape(block_total, comp_block, blocks_fp),
            footprint.reshape(block_total, comp_block, blocks_fp, voxels),
        ),
    )
    projected = jnp.transpose(pieces, (1, 0, 2)).reshape(frames_dev, comp_count)
    ordering = jnp.argsort(colour, stable=True)
    grouped = jnp.argsort(ordering)
    rank_in = grouped % quarter
    proj_group = projected[:, ordering].reshape(frames_dev, 4, quarter)
    gram_group = self_gram[ordering].reshape(4, quarter)
    nb_group = correlation[ordering].reshape(4, quarter, listed)
    weight_group = correlation_gram[ordering].reshape(4, quarter, listed)
    start_group = traces_init[:, ordering].reshape(frames_dev, 4, quarter)
    own_flat = colour * (tile_count * quarter) + tile_here * quarter + rank_in
    table, flat_all = (
        lax.all_gather(start_group, "tile", axis=2, tiled=True),
        lax.all_gather(own_flat, "tile", axis=0, tiled=True),
    )
    span_width = tile_count * quarter
    lookup = flat_all[nb_group]
    fresh_parts = []
    for step_colour in range(4):
        flat_table = table.reshape(frames_dev, 4 * span_width)
        values = jnp.take(flat_table, lookup[step_colour].reshape(-1), axis=1).reshape(
            frames_dev, quarter, listed
        )
        neighbour_sum = jnp.sum(values * weight_group[step_colour][None, :, :], axis=2)
        fresh = jnp.maximum(
            (proj_group[:, step_colour, :] - neighbour_sum) / gram_group[step_colour][None, :], 0.0
        )
        fresh_parts.append(fresh)
        if step_colour + 1 < 4:
            arrived_colour = lax.all_gather(fresh, "tile", axis=1, tiled=True)
            table = table.at[:, step_colour, :].set(arrived_colour)
    final_group = jnp.stack(fresh_parts, axis=1).reshape(frames_dev, comp_count)
    traces = final_group[:, grouped]
    energy_sum = lax.psum(jnp.sum(traces * traces, axis=0), "tm")
    trace_rms = jnp.sqrt(energy_sum / (frames_dev * lax.axis_size("tm")) + 1e-06)
    return (traces, trace_rms)


def solution(mesh):
    placed = (
        P("tile", "tm", None),
        P("tile", None, None),
        P("tile", None),
        P("tile", None, None),
        P("tile"),
        P("tile", None),
        P("tile", None),
        P("tm", "tile"),
    )
    return jax.shard_map(
        shards, mesh=mesh, in_specs=placed, out_specs=(P("tm", "tile"), P("tile")), check_vma=False
    )
```

profile of v0, /device:TPU:8, one launch (start us, length us, event | category | flops | bytes accessed | tf_op | source)
XLA Modules:
  0.0 362.0 jit_solution(10333032754767358957)
XLA Ops:
  0.7 0.8 copy.82
  1.5 0.1 reshape_squeeze.15
  1.6 2.4 gather_fusion
  4.0 13.8 %all-to-all-start = ((bf16[64,8,8,128]{3,2,1,0:T(8,128)(2,1)}), bf16[64,8,8,128]{3,2,1,0:T(8,128)(2,1)S(1)}, u32[]{:S(2)}, u32[]{:S(2)}) async-start(bf16[64,8,8,128]{3,2,1,0:T(8,128)(2,1)} %bitcast.2), calls=%async_computation | async-start | bytes 2097152 | tf_op jit(solution)/shard_map/all_to_all | solution.py:21
  17.9 1.0 multiply_reduce_fusion
  18.9 2.5 sort.34
  21.4 2.5 sort.35
  24.0 0.1 reshape.253
  24.1 0.1 copy.85
  24.2 1.2 gather_fusion.6
  25.4 0.6 gather_fusion.3
  26.1 0.1 reshape.338
  26.2 0.1 copy.87
  26.3 0.6 gather_fusion.5
  26.9 0.1 copy.86
  27.0 0.6 gather_fusion.2
  27.7 49.4 %all-gather = s32[64,1,128]{2,1,0:T(1,128)S(1)} all-gather(s32[1,1,128]{2,1,0:T(1,128)S(1)} %get-tuple-element.152), channel_id=1, replica_groups=mesh['tile'=64,'tm'=8] {'tile'}, dimensions={0}, use_global_device_ids=true | all-gather | bytes 33280 | tf_op jit(solution)/shard_map/all_gather | solution.py:57
  77.1 6.1 %gather_fusion.4 = s32[1024]{0:T(1024)S(1)} fusion(s32[8192]{0:T(1024)S(1)} %bitcast.154, s32[1024]{0:T(1024)S(1)} %broadcast_clamp_fusion), kind=kCustom, calls=%fused_computation.8 | custom fusion | bytes 12288 | tf_op jit(solution)/shard_map/gather | solution.py:60
  83.2 54.6 %all_gather.15 = f32[8,4,2048]{0,2,1:T(8,128)} all-gather(f32[8,4,32]{0,2,1:T(8,128)S(1)} %bitcast.173), channel_id=1, replica_groups=mesh['tile'=64,'tm'=8] {'tile'}, dimensions={2}, use_global_device_ids=true | all-gather | bytes 266240 | tf_op jit(solution)/shard_map/all_gather | solution.py:56
  137.8 2.9 gather_fusion.8
  140.8 0.1 fusion.10
  141.1 59.1 %while.14 = (s32[]{:T(128)}, f32[4,8,32]{2,1,0:T(8,128)S(1)}, bf16[4,32,8,128]{3,2,1,0:T(8,128)(2,1)S(1)}, s32[4,32,8]{1,0,2:T(4,128)S(1)}, bf16[512,8,128]{2,1,0:T(8,128)(2,1)S(1)}, /*index=5*/s32[]{:T(128)}) while((s32[]{:T(128)}, f32[4,8,32]{2,1,0:T(8,128)S(1)}, bf16[4,32,8,128]{3,2,1,0:T(8,128)(2,1)S(1)}, ...), condition=%wide.region_1.2_spmd.clone, body=%wide.region_0.0_spmd.clone.sunk | while | flops 67239936 | bytes 17915992 | solution.py:38
  141.1 0.1 copy.101
  141.2 3.3 convolution_bitcast_fusion.3
  144.4 8.0 %copy.102 = bf16[512,128,32]{1,2,0:T(8,128)(2,1)} copy(bf16[512,128,32]{0,1,2:T(8,128)(2,1)} %convolution_bitcast_fusion.3) | data formatting | bytes 8388608 | tf_op jit(solution)/shard_map/while/body/eval_jaxpr/kjs,kjv->svk/transpose | solution.py:33
  152.5 3.4 fusion.42
  155.9 3.3 convolution_bitcast_fusion.3
  159.2 8.0 %copy.102 = bf16[512,128,32]{1,2,0:T(8,128)(2,1)} copy(bf16[512,128,32]{0,1,2:T(8,128)(2,1)} %convolution_bitcast_fusion.3) | data formatting | bytes 8388608 | tf_op jit(solution)/shard_map/while/body/eval_jaxpr/kjs,kjv->svk/transpose | solution.py:33
  167.2 3.4 fusion.42
  170.7 3.3 convolution_bitcast_fusion.3
  174.0 8.0 %copy.102 = bf16[512,128,32]{1,2,0:T(8,128)(2,1)} copy(bf16[512,128,32]{0,1,2:T(8,128)(2,1)} %convolution_bitcast_fusion.3) | data formatting | bytes 8388608 | tf_op jit(solution)/shard_map/while/body/eval_jaxpr/kjs,kjv->svk/transpose | solution.py:33
  182.0 3.4 fusion.42
  185.5 3.3 convolution_bitcast_fusion.3
  188.8 8.0 %copy.102 = bf16[512,128,32]{1,2,0:T(8,128)(2,1)} copy(bf16[512,128,32]{0,1,2:T(8,128)(2,1)} %convolution_bitcast_fusion.3) | data formatting | bytes 8388608 | tf_op jit(solution)/shard_map/while/body/eval_jaxpr/kjs,kjv->svk/transpose | solution.py:33
  196.8 3.4 fusion.42
  200.2 0.1 copy.84
  200.2 0.7 gather_fusion.1
  200.9 0.1 fusion.25
  201.1 43.3 %all-gather.1 = f32[64,32,8]{1,2,0:T(8,128)S(1)} all-gather(f32[1,32,8]{1,2,0:T(8,128)S(1)} %copy.88), channel_id=1, replica_groups=mesh['tile'=64,'tm'=8] {'tile'}, dimensions={0}, use_global_device_ids=true | all-gather | bytes 66560 | tf_op jit(solution)/shard_map/all_gather | solution.py:73
  244.4 0.1 reshape.390
  244.5 0.3 copy.90
  244.8 1.1 constant_dynamic-update-slice_fusion.2
  245.9 2.9 gather_fusion.9
  248.8 0.1 fusion.9
  249.0 0.1 fusion.20
  249.1 42.1 %all-gather.2 = f32[64,32,8]{1,2,0:T(8,128)S(1)} all-gather(f32[1,32,8]{1,2,0:T(8,128)S(1)} %copy.91), channel_id=1, replica_groups=mesh['tile'=64,'tm'=8] {'tile'}, dimensions={0}, use_global_device_ids=true | all-gather | bytes 66560 | tf_op jit(solution)/shard_map/all_gather | solution.py:73
  291.3 0.1 reshape.392
  291.4 0.3 copy.93
  291.7 1.1 constant_dynamic-update-slice_fusion.1
  292.8 2.9 gather_fusion.10
  295.8 0.1 fusion.8
  295.9 0.1 fusion.15
  296.0 43.1 %all-gather.3 = f32[64,32,8]{1,2,0:T(8,128)S(1)} all-gather(f32[1,32,8]{1,2,0:T(8,128)S(1)} %copy.94), channel_id=1, replica_groups=mesh['tile'=64,'tm'=8] {'tile'}, dimensions={0}, use_global_device_ids=true | all-gather | bytes 66560 | tf_op jit(solution)/shard_map/all_gather | solution.py:73
  339.2 0.1 reshape.394
  339.3 0.3 copy.96
  339.7 1.1 constant_dynamic-update-slice_fusion
  340.7 2.9 gather_fusion.11
  343.6 0.1 fusion.7
  343.8 0.1 fusion.27
  343.9 0.6 gather_fusion.7
  344.5 0.1 multiply_reduce_fusion.1
  344.7 16.2 %psum.7 = f32[128]{0:T(128)S(1)} all-reduce(f32[128]{0:T(128)S(1)} %multiply_reduce_fusion.1), channel_id=1, replica_groups=mesh['tile'=64,'tm'=8] {'tm'}, use_global_device_ids=true, to_apply=%region_10.12 | all-reduce | flops 128 | bytes 1024 | tf_op jit(solution)/shard_map/psum | solution.py:77
  360.8 0.5 add_sqrt_fusion
  361.3 0.7 copy.97
  (47 shorter events, 0.9 us)
Async XLA Ops:
  0.6 1.0 copy-start
  0.6 17.2 %copy-start.1 = (bf16[128,8,128]{2,1,0:T(8,128)(2,1)S(1)}, bf16[128,8,128]{2,1,0:T(8,128)(2,1)}, u32[]{:S(2)}) copy-start(bf16[128,8,128]{2,1,0:T(8,128)(2,1)} %param.21) | copy-start | bytes 786436
  0.7 18.2 %copy-start.6 = (s32[128]{0:T(128)S(1)}, s32[128]{0:T(128)}, u32[]{:S(2)}) copy-start(s32[128]{0:T(128)} %param.22) | copy-start | bytes 1540
  0.7 23.3 %copy-start.2 = (s32[128,8]{0,1:T(8,128)S(1)}, s32[128,8]{0,1:T(8,128)}, u32[]{:S(2)}) copy-start(s32[128,8]{0,1:T(8,128)} %param.20) | copy-start | bytes 12292
  0.7 23.4 %copy-start.3 = (s32[128,8]{0,1:T(8,128)S(1)}, s32[128,8]{0,1:T(8,128)}, u32[]{:S(2)}) copy-start(s32[128,8]{0,1:T(8,128)} %param.23) | copy-start | bytes 12292
  0.7 25.5 %copy-start.4 = (f32[128,8]{0,1:T(8,128)S(1)}, f32[128,8]{0,1:T(8,128)}, u32[]{:S(2)}) copy-start(f32[128,8]{0,1:T(8,128)} %param.24) | copy-start | bytes 12292
  0.7 26.2 %copy-start.5 = (f32[8,128]{1,0:T(8,128)S(1)}, f32[8,128]{1,0:T(8,128)}, u32[]{:S(2)}) copy-start(f32[8,128]{1,0:T(8,128)} %param.25) | copy-start | bytes 12292
  4.0 137.0 %all-to-all-start = ((bf16[64,8,8,128]{3,2,1,0:T(8,128)(2,1)}), bf16[64,8,8,128]{3,2,1,0:T(8,128)(2,1)S(1)}, u32[]{:S(2)}, u32[]{:S(2)}) async-start(bf16[64,8,8,128]{3,2,1,0:T(8,128)(2,1)} %bitcast.2), calls=%async_computation | async-start | bytes 2097152 | tf_op jit(solution)/shard_map/all_to_all | solution.py:21
where the time goes:
time: 363 us; the launch traced here: 362 us
  blocking collectives  249 us (69%)
  local copies, waits for them, and re-layouts  64.4 us (18%)
  matrix products  26.6 us (7%)
  starting transfers between devices  13.8 us (4%)
  other arithmetic  7.73 us (2%)
    all_gather x3, blocking collectives, shards(): arrived_colour = lax.all_gather(fresh, 'tile', axis=1, tiled=True)  128 us
    all_gather x1, blocking collectives, shards(): lax.all_gather(start_group, 'tile', axis=2, tiled=True)  54.6 us
    all_gather x1, blocking collectives, shards(): lax.all_gather(own_flat, 'tile', axis=0, tiled=True)  49.4 us
    transpose x4, local copies, waits for them, and re-layouts, project(): jnp.einsum('kjs,kjv->svk', one_hot, weight_rows, preferred_element_type=j...  32.1 us
    psum x1, blocking collectives, shards(): energy_sum = lax.psum(jnp.sum(traces * traces, axis=0), 'tm')  16.2 us
    all_to_all x1, starting transfers between devices, shards(): lax.all_to_all(outgoing, 'tile', split_axis=0, concat_axis=0, tiled=True)  13.8 us
    dot_general x4, matrix products, project(): jnp.einsum('sfv,svk->fk', arrived, spread, preferred_element_type=jnp.flo...  13.5 us
    dot_general x4, matrix products, project(): jnp.einsum('kjs,kjv->svk', one_hot, weight_rows, preferred_element_type=j...  13.1 us
  transfers between devices with their start and end apart: 1, of which 0 were waited for; matrix products, arithmetic and copies ran while one was open for 5% of the time, Pallas kernels for 0%

commit v1 on v0

--- a/solution.py
+++ b/solution.py
@@ -52,8 +52,11 @@
     weight_group = correlation_gram[ordering].reshape(4, quarter, listed)
     start_group = traces_init[:, ordering].reshape(frames_dev, 4, quarter)
     own_flat = colour * (tile_count * quarter) + tile_here * quarter + rank_in
+    sites_pair = lambda v0: jnp.concatenate(
+        lax.all_to_all(jnp.stack(lax.axis_size("tile") * [v0], 0), "tile", 0, 0), 2
+    )
     table, flat_all = (
-        lax.all_gather(start_group, "tile", axis=2, tiled=True),
+        sites_pair(start_group),
         lax.all_gather(own_flat, "tile", axis=0, tiled=True),
     )
     span_width = tile_count * quarter

time: 363 us -> 338 us (0.931)
  blocking collectives: 249 us -> 186 us
  waiting for transfers between devices: 0.01 us -> 11.8 us
  local copies, waits for them, and re-layouts: 64.4 us -> 75.5 us
  starting transfers between devices: 13.8 us -> 20.5 us
  other arithmetic: 7.73 us -> 11.4 us
    all_gather x1 -> x0, blocking collectives: 54.6 us -> none  [shards(): lax.all_gather(start_group, 'tile', axis=2, tiled=True)]
    all_to_all x0 -> x1, starting transfers between devices: none -> 13.8 us  [shards(): lax.all_to_all(jnp.stack(lax.axis_size('tile') * [v0], 0), 'tile', 0, 0)]
    all_to_all x1, waiting for transfers between devices: 0.01 us -> 11.8 us  [shards(): lax.all_to_all(outgoing, 'tile', split_axis=0, concat_axis=0, tiled=True)]
    all_gather x1, blocking collectives: 49.4 us -> 41 us  [shards(): lax.all_gather(own_flat, 'tile', axis=0, tiled=True)]
    all_to_all x1, starting transfers between devices: 13.8 us -> 6.75 us  [shards(): lax.all_to_all(outgoing, 'tile', split_axis=0, concat_axis=0, tiled=True)]
    scatter x3 -> x6, local copies, waits for them, and re-layouts: 3.23 us -> 7.76 us  [shards(): table = table.at[:, step_colour, :].set(arrived_colour)]
    reshape x0 -> x4, local copies, waits for them, and re-layouts: none -> 3.84 us  [shards(): jnp.concatenate(lax.all_to_all(jnp.stack(lax.axis_size('tile') * [v0], 0)...]
  transfers between devices with their start and end apart: 1 -> 2, of which waited for: 0 -> 1; matrix products, arithmetic and copies ran while one was open for 5% -> 7% of each run, Pallas kernels for 0% -> 0%
where the time goes in v1:
time: 338 us; the launch traced here: 336 us
  blocking collectives  186 us (55%)
  local copies, waits for them, and re-layouts  75.5 us (22%)
  matrix products  29.7 us (9%)
  starting transfers between devices  20.5 us (6%)
  waiting for transfers between devices  11.8 us (3%)
  other arithmetic  11.4 us (3%)
    all_gather x3, blocking collectives, shards(): arrived_colour = lax.all_gather(fresh, 'tile', axis=1, tiled=True)  129 us
    all_gather x1, blocking collectives, shards(): lax.all_gather(own_flat, 'tile', axis=0, tiled=True)  41 us
    transpose x4, local copies, waits for them, and re-layouts, project(): jnp.einsum('kjs,kjv->svk', one_hot, weight_rows, preferred_element_type=j...  31.8 us
    dot_general x4, matrix products, project(): jnp.einsum('kjs,kjv->svk', one_hot, weight_rows, preferred_element_type=j...  16.2 us
    psum x1, blocking collectives, shards(): energy_sum = lax.psum(jnp.sum(traces * traces, axis=0), 'tm')  16.1 us
    all_to_all x1, starting transfers between devices, shards(): lax.all_to_all(jnp.stack(lax.axis_size('tile') * [v0], 0), 'tile', 0, 0)  13.8 us
    dot_general x4, matrix products, project(): jnp.einsum('sfv,svk->fk', arrived, spread, preferred_element_type=jnp.flo...  13.5 us
    all_to_all x1, waiting for transfers between devices, shards(): lax.all_to_all(outgoing, 'tile', split_axis=0, concat_axis=0, tiled=True)  11.8 us
  transfers between devices with their start and end apart: 2, of which 1 were waited for; matrix products, arithmetic and copies ran while one was open for 7% of the time, Pallas kernels for 0%

profile of v1, /device:TPU:8, one launch (start us, length us, event | category | flops | bytes accessed | tf_op | source)
XLA Modules:
  0.0 336.2 jit_solution(2289618944838083057)
XLA Ops:
  0.7 0.8 copy.94
  1.5 3.2 sort.34
  4.7 2.5 sort.35
  7.3 0.7 compare_select_fusion.7
  7.9 0.6 gather_fusion.2
  8.6 0.1 broadcast_bitcast_fusion
  8.8 1.2 reshape.406
  9.9 13.8 %all-to-all-start.1 = ((f32[64,1,1024]{2,1,0:T(1,128)}), f32[64,1,1024]{2,1,0:T(1,128)S(1)}, u32[]{:S(2)}, u32[]{:S(2)}) async-start(f32[64,1,1024]{2,1,0:T(1,128)} %reshape.406), calls=%async_computation.1 | async-start | bytes 524288 | tf_op jit(solution)/shard_map/all_to_all | solution.py:56
  23.7 0.8 copy.93
  24.5 0.6 gather_fusion.3
  25.3 0.8 copy.97
  26.1 0.6 gather_fusion.5
  27.0 1.0 multiply_reduce_fusion
  28.0 1.2 gather_fusion.6
  29.3 2.4 gather_fusion
  31.7 41.0 %all-gather = s32[64,1,128]{2,1,0:T(1,128)S(1)} all-gather(s32[1,1,128]{2,1,0:T(1,128)S(1)} %get-tuple-element.152), channel_id=1, replica_groups=mesh['tile'=64,'tm'=8] {'tile'}, dimensions={0}, use_global_device_ids=true | all-gather | bytes 33280 | tf_op jit(solution)/shard_map/all_gather | solution.py:60
  72.7 6.8 %all-to-all-start = ((bf16[64,8,8,128]{3,2,1,0:T(8,128)(2,1)}), bf16[64,8,8,128]{3,2,1,0:T(8,128)(2,1)S(1)}, u32[]{:S(2)}, u32[]{:S(2)}) async-start(bf16[64,8,8,128]{3,2,1,0:T(8,128)(2,1)} %bitcast.2), calls=%async_computation | async-start | bytes 2097152 | tf_op jit(solution)/shard_map/all_to_all | solution.py:21
  79.4 6.2 %gather_fusion.4 = s32[1024]{0:T(1024)S(1)} fusion(s32[8192]{0:T(1024)S(1)} %bitcast.167, s32[1024]{0:T(1024)S(1)} %broadcast_clamp_fusion), kind=kCustom, calls=%fused_computation.8 | custom fusion | bytes 12288 | tf_op jit(solution)/shard_map/gather | solution.py:63
  85.7 0.6 fusion.32
  86.2 0.5 compare_and_fusion
  86.8 0.5 broadcast.200
  87.3 1.3 reduce.6
  88.5 0.3 reshape.407
  89.0 2.7 copy.96
  91.6 0.6 copy.98
  92.3 0.5 reshape.263
  92.7 2.9 gather_fusion.8
  95.7 0.8 fusion.10
  96.5 11.8 %all-to-all-done = bf16[64,8,8,128]{3,2,1,0:T(8,128)(2,1)S(1)} async-done(((bf16[64,8,8,128]{3,2,1,0:T(8,128)(2,1)}), bf16[64,8,8,128]{3,2,1,0:T(8,128)(2,1)S(1)}, u32[]{:S(2)}, u32[]{:S(2)}) %all-to-all-start) | async-done | bytes 1048608 | tf_op jit(solution)/shard_map/all_to_all | solution.py:21
  108.3 61.9 %while.14 = (s32[]{:T(128)}, f32[4,8,32]{2,1,0:T(8,128)S(1)}, bf16[4,32,8,128]{3,2,1,0:T(8,128)(2,1)}, s32[4,32,8]{1,0,2:T(4,128)S(1)}, bf16[512,8,128]{2,1,0:T(8,128)(2,1)S(1)}, /*index=5*/s32[]{:T(128)}) while((s32[]{:T(128)}, f32[4,8,32]{2,1,0:T(8,128)S(1)}, bf16[4,32,8,128]{3,2,1,0:T(8,128)(2,1)}, s32[4,32,8]{1,0,2:T(4,128)S(1)}, ...), condition=%wide.region_1.2_spmd.clone, body=%wide.region_0.0_spmd.clone.sunk | while | flops 67239936 | bytes 17900632 | solution.py:38
  108.4 4.1 %convolution_bitcast_fusion.3 = bf16[512,128,32]{0,1,2:T(8,128)(2,1)} fusion(s32[32,8]{1,0:T(8,128)S(1)} %copy.112, bf16[4,32,8,128]{3,2,1,0:T(8,128)(2,1)} %get-tuple-element.203, s32[]{:T(128)S(6)} %copy.117), kind=kOutput, calls=%fused_computation.13.clone.1 | convolution fusion | flops 33685504 | bytes 4260868 | tf_op jit(solution)/shard_map/while/body/eval_jaxpr/kjs,kjv->svk/dot_general | solution.py:33
  112.4 8.0 %copy.113 = bf16[512,128,32]{1,2,0:T(8,128)(2,1)} copy(bf16[512,128,32]{0,1,2:T(8,128)(2,1)} %convolution_bitcast_fusion.3) | data formatting | bytes 8388608 | tf_op jit(solution)/shard_map/while/body/eval_jaxpr/kjs,kjv->svk/transpose | solution.py:33
  120.4 3.4 %fusion.42 = f32[4,8,32]{2,1,0:T(8,128)S(1)} fusion(f32[4,8,32]{2,1,0:T(8,128)S(1)} %get-tuple-element.196, s32[]{:T(128)S(6)} %copy.117, bf16[512,128,32]{1,2,0:T(8,128)(2,1)} %copy.113, bf16[512,8,128]{2,1,0:T(8,128)(2,1)S(1)} %get-tuple-element.205), kind=kOutput, calls=%fused_computation.15.clone.1 | convolution fusion | flops 33554432 | bytes 5246980 | tf_op jit(solution)/shard_map/while/body/eval_jaxpr/sfv,svk->fk/dot_general | solution.py:36
  123.9 4.1 %convolution_bitcast_fusion.3 = bf16[512,128,32]{0,1,2:T(8,128)(2,1)} fusion(s32[32,8]{1,0:T(8,128)S(1)} %copy.112, bf16[4,32,8,128]{3,2,1,0:T(8,128)(2,1)} %get-tuple-element.203, s32[]{:T(128)S(6)} %copy.117), kind=kOutput, calls=%fused_computation.13.clone.1 | convolution fusion | flops 33685504 | bytes 4260868 | tf_op jit(solution)/shard_map/while/body/eval_jaxpr/kjs,kjv->svk/dot_general | solution.py:33
  127.9 8.0 %copy.113 = bf16[512,128,32]{1,2,0:T(8,128)(2,1)} copy(bf16[512,128,32]{0,1,2:T(8,128)(2,1)} %convolution_bitcast_fusion.3) | data formatting | bytes 8388608 | tf_op jit(solution)/shard_map/while/body/eval_jaxpr/kjs,kjv->svk/transpose | solution.py:33
  135.9 3.4 %fusion.42 = f32[4,8,32]{2,1,0:T(8,128)S(1)} fusion(f32[4,8,32]{2,1,0:T(8,128)S(1)} %get-tuple-element.196, s32[]{:T(128)S(6)} %copy.117, bf16[512,128,32]{1,2,0:T(8,128)(2,1)} %copy.113, bf16[512,8,128]{2,1,0:T(8,128)(2,1)S(1)} %get-tuple-element.205), kind=kOutput, calls=%fused_computation.15.clone.1 | convolution fusion | flops 33554432 | bytes 5246980 | tf_op jit(solution)/shard_map/while/body/eval_jaxpr/sfv,svk->fk/dot_general | solution.py:36
  139.4 4.1 %convolution_bitcast_fusion.3 = bf16[512,128,32]{0,1,2:T(8,128)(2,1)} fusion(s32[32,8]{1,0:T(8,128)S(1)} %copy.112, bf16[4,32,8,128]{3,2,1,0:T(8,128)(2,1)} %get-tuple-element.203, s32[]{:T(128)S(6)} %copy.117), kind=kOutput, calls=%fused_computation.13.clone.1 | convolution fusion | flops 33685504 | bytes 4260868 | tf_op jit(solution)/shard_map/while/body/eval_jaxpr/kjs,kjv->svk/dot_general | solution.py:33
  143.4 8.0 %copy.113 = bf16[512,128,32]{1,2,0:T(8,128)(2,1)} copy(bf16[512,128,32]{0,1,2:T(8,128)(2,1)} %convolution_bitcast_fusion.3) | data formatting | bytes 8388608 | tf_op jit(solution)/shard_map/while/body/eval_jaxpr/kjs,kjv->svk/transpose | solution.py:33
  151.4 3.4 %fusion.42 = f32[4,8,32]{2,1,0:T(8,128)S(1)} fusion(f32[4,8,32]{2,1,0:T(8,128)S(1)} %get-tuple-element.196, s32[]{:T(128)S(6)} %copy.117, bf16[512,128,32]{1,2,0:T(8,128)(2,1)} %copy.113, bf16[512,8,128]{2,1,0:T(8,128)(2,1)S(1)} %get-tuple-element.205), kind=kOutput, calls=%fused_computation.15.clone.1 | convolution fusion | flops 33554432 | bytes 5246980 | tf_op jit(solution)/shard_map/while/body/eval_jaxpr/sfv,svk->fk/dot_general | solution.py:36
  154.8 4.1 %convolution_bitcast_fusion.3 = bf16[512,128,32]{0,1,2:T(8,128)(2,1)} fusion(s32[32,8]{1,0:T(8,128)S(1)} %copy.112, bf16[4,32,8,128]{3,2,1,0:T(8,128)(2,1)} %get-tuple-element.203, s32[]{:T(128)S(6)} %copy.117), kind=kOutput, calls=%fused_computation.13.clone.1 | convolution fusion | flops 33685504 | bytes 4260868 | tf_op jit(solution)/shard_map/while/body/eval_jaxpr/kjs,kjv->svk/dot_general | solution.py:33
  158.9 8.0 %copy.113 = bf16[512,128,32]{1,2,0:T(8,128)(2,1)} copy(bf16[512,128,32]{0,1,2:T(8,128)(2,1)} %convolution_bitcast_fusion.3) | data formatting | bytes 8388608 | tf_op jit(solution)/shard_map/while/body/eval_jaxpr/kjs,kjv->svk/transpose | solution.py:33
  166.9 3.4 %fusion.42 = f32[4,8,32]{2,1,0:T(8,128)S(1)} fusion(f32[4,8,32]{2,1,0:T(8,128)S(1)} %get-tuple-element.196, s32[]{:T(128)S(6)} %copy.117, bf16[512,128,32]{1,2,0:T(8,128)(2,1)} %copy.113, bf16[512,8,128]{2,1,0:T(8,128)(2,1)S(1)} %get-tuple-element.205), kind=kOutput, calls=%fused_computation.15.clone.1 | convolution fusion | flops 33554432 | bytes 5246980 | tf_op jit(solution)/shard_map/while/body/eval_jaxpr/sfv,svk->fk/dot_general | solution.py:36
  170.3 0.7 gather_fusion.1
  171.1 43.9 %all-gather.1 = f32[64,32,8]{1,2,0:T(8,128)S(1)} all-gather(f32[1,32,8]{1,2,0:T(8,128)S(1)} %copy.99), channel_id=1, replica_groups=mesh['tile'=64,'tm'=8] {'tile'}, dimensions={0}, use_global_device_ids=true | all-gather | bytes 66560 | tf_op jit(solution)/shard_map/all_gather | solution.py:76
  215.1 0.1 reshape.392
  215.2 2.6 copy.101
  217.8 2.9 gather_fusion.9
  220.7 0.1 fusion.9
  221.0 41.8 %all-gather.2 = f32[64,32,8]{1,2,0:T(8,128)S(1)} all-gather(f32[1,32,8]{1,2,0:T(8,128)S(1)} %copy.102), channel_id=1, replica_groups=mesh['tile'=64,'tm'=8] {'tile'}, dimensions={0}, use_global_device_ids=true | all-gather | bytes 66560 | tf_op jit(solution)/shard_map/all_gather | solution.py:76
  262.8 0.1 reshape.394
  263.0 2.6 copy.104
  265.6 2.9 gather_fusion.10
  268.5 0.1 fusion.8
  268.8 43.4 %all-gather.3 = f32[64,32,8]{1,2,0:T(8,128)S(1)} all-gather(f32[1,32,8]{1,2,0:T(8,128)S(1)} %copy.105), channel_id=1, replica_groups=mesh['tile'=64,'tm'=8] {'tile'}, dimensions={0}, use_global_device_ids=true | all-gather | bytes 66560 | tf_op jit(solution)/shard_map/all_gather | solution.py:76
  312.2 0.1 reshape.396
  312.4 2.6 copy.107
  315.0 2.9 gather_fusion.11
  317.9 0.1 fusion.7
  318.0 0.1 fusion.27
  318.1 0.6 gather_fusion.7
  318.8 0.1 multiply_reduce_fusion.1
  318.9 0.7 copy.108
  319.6 16.1 %psum.7 = f32[128]{0:T(128)S(1)} all-reduce(f32[128]{0:T(128)S(1)} %multiply_reduce_fusion.1), channel_id=1, replica_groups=mesh['tile'=64,'tm'=8] {'tm'}, use_global_device_ids=true, to_apply=%region_10.12 | all-reduce | flops 128 | bytes 1024 | tf_op jit(solution)/shard_map/psum | solution.py:80
  335.7 0.5 add_sqrt_fusion
  (54 shorter events, 1.7 us)
Async XLA Ops:
  0.6 28.6 %copy-start = (bf16[128,8,128]{2,1,0:T(8,128)(2,1)S(1)}, bf16[128,8,128]{2,1,0:T(8,128)(2,1)}, u32[]{:S(2)}) copy-start(bf16[128,8,128]{2,1,0:T(8,128)(2,1)} %param.18) | copy-start | bytes 786436
  0.6 26.1 %copy-start.2 = (s32[128,8]{0,1:T(8,128)S(1)}, s32[128,8]{0,1:T(8,128)}, u32[]{:S(2)}) copy-start(s32[128,8]{0,1:T(8,128)} %param.20) | copy-start | bytes 12292
  0.7 26.1 %copy-start.3 = (s32[1,64,8]{1,2,0:T(8,128)S(1)}, s32[1,64,8]{1,2,0:T(8,128)}, u32[]{:S(2)}) copy-start(s32[1,64,8]{1,2,0:T(8,128)} %param.19) | copy-start | bytes 6148
  0.7 26.3 %copy-start.1 = (bf16[128,8,128]{2,1,0:T(8,128)(2,1)S(1)}, bf16[128,8,128]{2,1,0:T(8,128)(2,1)}, u32[]{:S(2)}) copy-start(bf16[128,8,128]{2,1,0:T(8,128)(2,1)} %param.21) | copy-start | bytes 786436
  9.9 62.7 %all-to-all-start.1 = ((f32[64,1,1024]{2,1,0:T(1,128)}), f32[64,1,1024]{2,1,0:T(1,128)S(1)}, u32[]{:S(2)}, u32[]{:S(2)}) async-start(f32[64,1,1024]{2,1,0:T(1,128)} %reshape.406), calls=%async_computation.1 | async-start | bytes 524288 | tf_op jit(solution)/shard_map/all_to_all | solution.py:56
  72.7 35.6 %all-to-all-start = ((bf16[64,8,8,128]{3,2,1,0:T(8,128)(2,1)}), bf16[64,8,8,128]{3,2,1,0:T(8,128)(2,1)S(1)}, u32[]{:S(2)}, u32[]{:S(2)}) async-start(bf16[64,8,8,128]{3,2,1,0:T(8,128)(2,1)} %bitcast.2), calls=%async_computation | async-start | bytes 2097152 | tf_op jit(solution)/shard_map/all_to_all | solution.py:21
  265.6 52.4 %copy-start.4 = (f32[32]{0:T(128)S(1)}, f32[32]{0:T(128)}, u32[]{:S(2)}) copy-start(f32[32]{0:T(128)} %get-tuple-element.153) | copy-start | bytes 388
